TPU v7x, 512 devices: a whole 4x4x16 slice. The times are simulated.
512 devices in a mesh: tm: 64 (over y, z), head: 8 (over x, core).
Axes of the slice: x: 4, y: 4, z: 16, core: 2. Of those that a mesh axis runs over, the one named last changes fastest.
Arguments:
- queries: bfloat16 [16384, 3072], P('tm', 'head'), may hold values from -170 to 170
- key_rows: bfloat16 [16384, 3072], P('tm', 'head'), may hold values from -6 to 6
- value_rows: bfloat16 [16384, 3072], P('tm', 'head'), may hold values from -102 to 102
- grad_normed: bfloat16 [16384, 3072], P('tm', 'head'), may hold values from -5.5 to 5.5
- norm_gain: float32 [3072], P('head'), may hold values from 0.25 to 1.75
- utter_ids: int32 [128], P('tm'), may hold values from 0 to 20, never falling along the last dimension, each value on 1 to 8 neighbouring positions
Outputs:
- normed: bfloat16 [16384, 3072], P('tm', 'head')
- grad_queries: bfloat16 [16384, 3072], P('tm', 'head')
- grad_keys: bfloat16 [16384, 3072], P('tm', 'head')
- grad_values: bfloat16 [16384, 3072], P('tm', 'head')
- grad_gain: float32 [3072], P('head')
Inputs may be any that keep to these rules, and one draw needn't show every extreme that they name: `utter_ids`: ids never fall; each utterance covers 1 to 8 consecutive blocks of 128 frames, and one covers exactly 8.
All inputs are finite; a program needn't handle non-finite values.
Results may differ from a plain program's by a relative error of at most 0.024.
Values may be sent and summed in bfloat16 or wider, within the bound.
A program may use at most 64 MiB of HBM per device.

v0:
```python
import jax
import jax.numpy as jnp
from jax import lax
from jax.sharding import PartitionSpec as P

HSZ = 128
REACH = 4


def for_sending(x):

    def short(part):
        return part.astype(jnp.bfloat16) if part.dtype == jnp.float32 else part

    return jax.tree.map(short, x)


def passed_along(x, axis, by):
    length = lax.axis_size(axis)
    pairs = [(i, i + by) for i in range(length) if 0 <= i + by < length]
    return lax.ppermute(x, axis, pairs)


def frame_utter(utter_ids, row_count):
    blocks = utter_ids.shape[0]
    spread = jnp.broadcast_to(utter_ids[:, None] + 1, (blocks, row_count // blocks))
    return spread.reshape(row_count)


def rounded_term(term):
    return lax.optimization_barrier(term.astype(jnp.bfloat16)).astype(jnp.float32)


def tile_scores(query_heads, key_heads, query_utt, key_utt, factor):
    scores = (
        jnp.einsum("qhe,khe->hqk", query_heads, key_heads, preferred_element_type=jnp.float32)
        * factor
    )
    allowed = query_utt[:, None] == key_utt[None, :]
    return jnp.where(allowed[None], scores, -jnp.inf)


def lse_step(query_heads, query_utt, key_heads, key_utt, factor, current):
    top_score, exp_total = current
    scores = tile_scores(query_heads, key_heads, query_utt, key_utt, factor)
    new_top = jnp.maximum(top_score, jnp.max(scores, axis=2))
    exp_total = exp_total * jnp.exp(top_score - new_top) + jnp.sum(
        jnp.exp(scores - new_top[:, :, None]), axis=2
    )
    return (new_top, exp_total)


def output_step(
    query_heads, query_utt, key_heads, value_heads, key_utt, log_total, factor, out_accum
):
    weights = jnp.exp(
        tile_scores(query_heads, key_heads, query_utt, key_utt, factor) - log_total[:, :, None]
    )
    return out_accum + jnp.einsum(
        "hqk,khe->qhe",
        weights.astype(jnp.bfloat16),
        value_heads,
        preferred_element_type=jnp.float32,
    )


def tile_grads(
    query_heads,
    grad_heads,
    key_heads,
    value_heads,
    query_utt,
    key_utt,
    log_total,
    row_delta,
    factor,
):
    scores = tile_scores(query_heads, key_heads, query_utt, key_utt, factor)
    weights = jnp.exp(scores - log_total[:, :, None])
    grad_weights = jnp.einsum(
        "qhe,khe->hqk", grad_heads, value_heads, preferred_element_type=jnp.float32
    )
    dscore = (weights * (grad_weights - row_delta[:, :, None])).astype(jnp.bfloat16)
    return (weights.astype(jnp.bfloat16), dscore)


def query_step(
    query_heads,
    grad_heads,
    key_heads,
    value_heads,
    query_utt,
    key_utt,
    log_total,
    row_delta,
    factor,
    current,
):
    weights_b, dscore = tile_grads(
        query_heads,
        grad_heads,
        key_heads,
        value_heads,
        query_utt,
        key_utt,
        log_total,
        row_delta,
        factor,
    )
    grad_query = (
        current[0]
        + jnp.einsum("hqk,khe->qhe", dscore, key_heads, preferred_element_type=jnp.float32) * factor
    )
    key_grad = (
        jnp.einsum("hqk,qhe->khe", dscore, query_heads, preferred_element_type=jnp.float32) * factor
    )
    value_grad = jnp.einsum(
        "hqk,qhe->khe", weights_b, grad_heads, preferred_element_type=jnp.float32
    )
    return (grad_query, key_grad, value_grad)


def body(queries, key_rows, value_rows, grad_normed, norm_gain, utter_ids):
    row_count, feat_width = queries.shape
    head_count = feat_width // HSZ
    factor = HSZ ** (-0.5)
    layout = (row_count, head_count, HSZ)
    query_heads = queries.reshape(layout)
    own_utt = frame_utter(utter_ids, row_count)
    own_pair = jnp.stack([key_rows, value_rows])
    sources = [(own_pair, own_utt)]
    moving = (own_pair, own_utt)
    for distance in range(REACH):
        moving = passed_along((moving[0], for_sending(moving[1])), "tm", 1)
        sources.append(moving)
    key_blocks = []
    for source in sources:
        pair_rows = source[0]
        key_utt = source[1]
        live = jnp.any(own_utt[:, None] == key_utt[None, :])
        key_blocks.append(
            (pair_rows[0].reshape(layout), pair_rows[1].reshape(layout), key_utt, live)
        )
    top_score = jnp.full((head_count, row_count), -jnp.inf, jnp.float32)
    exp_total = jnp.zeros((head_count, row_count), jnp.float32)
    for key_block in key_blocks:
        top_score, exp_total = lse_step(
            query_heads, own_utt, key_block[0], key_block[2], factor, (top_score, exp_total)
        )
    log_total = top_score + jnp.log(exp_total)
    out_accum = jnp.zeros(layout, jnp.float32)
    for key_block in key_blocks:
        out_accum = output_step(
            query_heads,
            own_utt,
            key_block[0],
            key_block[1],
            key_block[2],
            log_total,
            factor,
            out_accum,
        )
    attended = out_accum.astype(jnp.bfloat16)
    flat_att = attended.reshape(row_count, feat_width).astype(jnp.float32)
    features = feat_width * lax.axis_size("head")
    grad_rows = grad_normed.astype(jnp.float32)
    scaled = grad_rows * norm_gain
    square_sum, cross_sum = lax.psum(
        (jnp.sum(flat_att * flat_att, axis=1), jnp.sum(scaled * flat_att, axis=1)), "head"
    )
    rms_inv = 1.0 / jnp.sqrt(square_sum / features + 1e-06)
    normed = (flat_att * rms_inv[:, None] * norm_gain).astype(jnp.bfloat16)
    grad_att = (
        rms_inv[:, None] * (scaled - flat_att * (rms_inv * rms_inv * cross_sum / features)[:, None])
    ).astype(jnp.bfloat16)
    grad_gain = lax.psum(jnp.sum(grad_rows * flat_att * rms_inv[:, None], axis=0), "tm")
    grad_heads = grad_att.reshape(layout)
    row_delta = jnp.sum(attended.astype(jnp.float32) * grad_heads.astype(jnp.float32), axis=2).T
    zero_heads = jnp.zeros(layout, jnp.float32)
    grad_query = zero_heads
    key_parts = []
    for key_block in key_blocks:
        grad_query, key_grad, value_grad = query_step(
            query_heads,
            grad_heads,
            key_block[0],
            key_block[1],
            own_utt,
            key_block[2],
            log_total,
            row_delta,
            factor,
            (grad_query, zero_heads, zero_heads),
        )
        key_parts.append(
            jnp.stack(
                [key_grad.reshape(row_count, feat_width), value_grad.reshape(row_count, feat_width)]
            )
        )
    carried = rounded_term(key_parts[0])
    for distance in range(1, REACH + 1):
        arrived = passed_along(key_parts[distance].astype(jnp.bfloat16), "tm", -distance)
        carried = carried + arrived.astype(jnp.float32)
    grad_queries = grad_query.reshape(row_count, feat_width).astype(jnp.bfloat16)
    return (
        normed,
        grad_queries,
        carried[0].astype(jnp.bfloat16),
        carried[1].astype(jnp.bfloat16),
        grad_gain,
    )


def solution(mesh):
    in_specs = (
        P("tm", "head"),
        P("tm", "head"),
        P("tm", "head"),
        P("tm", "head"),
        P("head"),
        P("tm"),
    )
    out_specs = (P("tm", "head"), P("tm", "head"), P("tm", "head"), P("tm", "head"), P("head"))
    return jax.shard_map(body, mesh=mesh, in_specs=in_specs, out_specs=out_specs, check_vma=False)
```

profile of v0, /device:TPU:6, one launch (start us, length us, event | category | flops | bytes accessed | tf_op | source)
XLA Modules:
  0.0 350.9 jit_solution(14660419836064884476)
XLA Ops:
  1.4 3.9 %collective-permute-start = (s32[256]{0:T(256)S(1)}, s32[256]{0:T(256)S(1)}, u32[]{:S(2)}, u32[]{:S(2)}) collective-permute-start(s32[256]{0:T(256)S(1)} %broadcast_bitcast_fusion), channel_id=1, source_target_pairs={{0,8},{8,16},{16,24},{24,32},{32,40},{40,48},{48,56},{56,64},{64,7... | collective-permute-start | bytes 3080 | tf_op jit(solution)/shard_map/ppermute | solution.py:21
  5.3 1.3 collective-permute-done
  6.6 4.2 %collective-permute-start.2 = (s32[256]{0:T(256)S(1)}, s32[256]{0:T(256)S(1)}, u32[]{:S(2)}, u32[]{:S(2)}) collective-permute-start(s32[256]{0:T(256)S(1)} %collective-permute-done), channel_id=1, source_target_pairs={{0,8},{8,16},{16,24},{24,32},{32,40},{40,48},{48,56},{56,64},{64,7... | collective-permute-start | bytes 3080 | tf_op jit(solution)/shard_map/ppermute | solution.py:21
  10.8 1.3 collective-permute-done.2
  12.0 4.2 %collective-permute-start.4 = (s32[256]{0:T(256)S(1)}, s32[256]{0:T(256)S(1)}, u32[]{:S(2)}, u32[]{:S(2)}) collective-permute-start(s32[256]{0:T(256)S(1)} %collective-permute-done.2), channel_id=1, source_target_pairs={{0,8},{8,16},{16,24},{24,32},{32,40},{40,48},{48,56},{56,64},{64,7... | collective-permute-start | bytes 3080 | tf_op jit(solution)/shard_map/ppermute | solution.py:21
  16.2 1.1 copy.85
  17.5 4.3 %collective-permute-start.6 = (s32[256]{0:T(256)S(1)}, s32[256]{0:T(256)S(1)}, u32[]{:S(2)}, u32[]{:S(2)}) collective-permute-start(s32[256]{0:T(256)S(1)} %collective-permute-done.4), channel_id=1, source_target_pairs={{0,8},{8,16},{16,24},{24,32},{32,40},{40,48},{48,56},{56,64},{64,7... | collective-permute-start | bytes 3080 | tf_op jit(solution)/shard_map/ppermute | solution.py:21
  21.9 5.5 %collective-permute-start.1 = (bf16[2,256,384]{1,2,0:T(8,128)(2,1)S(1)}, bf16[2,256,384]{1,2,0:T(8,128)(2,1)S(1)}, u32[]{:S(2)}, u32[]{:S(2)}) collective-permute-start(bf16[2,256,384]{1,2,0:T(8,128)(2,1)S(1)} %pad_maximum_fusion), channel_id=1, source_target_pairs={{0,8},{8,16},{16,24},{24,32},{32,40},{40,48},{48,56},{56,64},{64,7... | collective-permute-start | bytes 1179656 | tf_op jit(solution)/shard_map/ppermute | solution.py:21
  28.4 4.8 %collective-permute-done.1 = bf16[2,256,384]{1,2,0:T(8,128)(2,1)S(1)} collective-permute-done((bf16[2,256,384]{1,2,0:T(8,128)(2,1)S(1)}, bf16[2,256,384]{1,2,0:T(8,128)(2,1)S(1)}, u32[]{:S(2)}, u32[]{:S(2)}) %collective-permute-start.1) | collective-permute-done | bytes 393248 | tf_op jit(solution)/shard_map/ppermute | solution.py:21
  33.2 5.1 %collective-permute-start.3 = (bf16[2,256,384]{1,2,0:T(8,128)(2,1)S(1)}, bf16[2,256,384]{1,2,0:T(8,128)(2,1)S(1)}, u32[]{:S(2)}, u32[]{:S(2)}) collective-permute-start(bf16[2,256,384]{1,2,0:T(8,128)(2,1)S(1)} %collective-permute-done.1), channel_id=1, source_target_pairs={{0,8},{8,16},{16,24},{24,32},{32,40},{40,48},{48,56},{56,64},{64,7... | collective-permute-start | bytes 1179656 | tf_op jit(solution)/shard_map/ppermute | solution.py:21
  39.0 4.8 %collective-permute-done.3 = bf16[2,256,384]{1,2,0:T(8,128)(2,1)S(1)} collective-permute-done((bf16[2,256,384]{1,2,0:T(8,128)(2,1)S(1)}, bf16[2,256,384]{1,2,0:T(8,128)(2,1)S(1)}, u32[]{:S(2)}, u32[]{:S(2)}) %collective-permute-start.3) | collective-permute-done | bytes 393248 | tf_op jit(solution)/shard_map/ppermute | solution.py:21
  43.8 6.7 %collective-permute-start.5 = (bf16[2,256,384]{1,2,0:T(8,128)(2,1)S(1)}, bf16[2,256,384]{1,2,0:T(8,128)(2,1)S(1)}, u32[]{:S(2)}, u32[]{:S(2)}) collective-permute-start(bf16[2,256,384]{1,2,0:T(8,128)(2,1)S(1)} %collective-permute-done.3), channel_id=1, source_target_pairs={{0,8},{8,16},{16,24},{24,32},{32,40},{40,48},{48,56},{56,64},{64,7... | collective-permute-start | bytes 1179656 | tf_op jit(solution)/shard_map/ppermute | solution.py:21
  51.2 6.6 %collective-permute-done.5 = bf16[2,256,384]{1,2,0:T(8,128)(2,1)S(1)} collective-permute-done((bf16[2,256,384]{1,2,0:T(8,128)(2,1)S(1)}, bf16[2,256,384]{1,2,0:T(8,128)(2,1)S(1)}, u32[]{:S(2)}, u32[]{:S(2)}) %collective-permute-start.5) | collective-permute-done | bytes 393248 | tf_op jit(solution)/shard_map/ppermute | solution.py:21
  57.9 5.0 %collective-permute-start.7 = (bf16[2,256,384]{1,2,0:T(8,128)(2,1)S(1)}, bf16[2,256,384]{1,2,0:T(8,128)(2,1)S(1)}, u32[]{:S(2)}, u32[]{:S(2)}) collective-permute-start(bf16[2,256,384]{1,2,0:T(8,128)(2,1)S(1)} %collective-permute-done.5), channel_id=1, source_target_pairs={{0,8},{8,16},{16,24},{24,32},{32,40},{40,48},{48,56},{56,64},{64,7... | collective-permute-start | bytes 1179656 | tf_op jit(solution)/shard_map/ppermute | solution.py:21
  63.6 4.5 %collective-permute-done.7 = bf16[2,256,384]{1,2,0:T(8,128)(2,1)S(1)} collective-permute-done((bf16[2,256,384]{1,2,0:T(8,128)(2,1)S(1)}, bf16[2,256,384]{1,2,0:T(8,128)(2,1)S(1)}, u32[]{:S(2)}, u32[]{:S(2)}) %collective-permute-start.7) | collective-permute-done | bytes 393248 | tf_op jit(solution)/shard_map/ppermute | solution.py:21
  70.8 1.1 multiply_reduce_fusion.1
  71.8 10.0 %psum.21 = f32[256]{0:T(256)S(1)} all-reduce(f32[256]{0:T(256)S(1)} %get-tuple-element.48), channel_id=1, replica_groups=mesh['tm'=64,'head'=8] {'head'}, use_global_device_ids=true, to_apply=%region_11.12 | all-reduce | flops 256 | bytes 2048 | tf_op jit(solution)/shard_map/psum | solution.py:168
  81.8 2.0 copy.105
  83.8 1.7 fusion.47
  85.5 12.0 %psum.22 = f32[256]{0:T(256)} all-reduce(f32[256]{0:T(256)} %get-tuple-element.16), channel_id=1, replica_groups=mesh['tm'=64,'head'=8] {'head'}, use_global_device_ids=true, to_apply=%region_13.14 | all-reduce | flops 256 | bytes 2048 | tf_op jit(solution)/shard_map/psum | solution.py:168
  98.3 1.9 fusion.45
  100.2 1.1 copy.108
  101.2 1.1 multiply_reduce_fusion
  102.3 1.0 convolution_convert_fusion.3
  103.4 1.1 fusion.11
  104.5 1.1 fusion.12
  121.3 1.3 collective-permute-start.8
  123.4 1.3 collective-permute-start.9
  125.5 1.4 collective-permute-start.11
  127.7 1.3 collective-permute-start.10
  131.4 217.4 %psum.23 = f32[384]{0:T(512)} all-reduce(f32[384]{0:T(512)S(1)} %copy-done.40), channel_id=1, replica_groups=mesh['tm'=64,'head'=8] {'tm'}, use_global_device_ids=true, to_apply=%region_16.17 | all-reduce | flops 384 | bytes 3072 | tf_op jit(solution)/shard_map/psum | solution.py:176
  348.8 1.2 add_convert_fusion
  (148 shorter events, 28.2 us)
Async XLA Ops:
  1.4 15.9 %copy-start.37 = (bf16[256,384]{1,0:T(8,128)(2,1)S(1)}, bf16[256,384]{1,0:T(8,128)(2,1)}, u32[]{:S(2)}) copy-start(bf16[256,384]{1,0:T(8,128)(2,1)} %param.8) | copy-start | bytes 589828
  1.4 5.2 %collective-permute-start = (s32[256]{0:T(256)S(1)}, s32[256]{0:T(256)S(1)}, u32[]{:S(2)}, u32[]{:S(2)}) collective-permute-start(s32[256]{0:T(256)S(1)} %broadcast_bitcast_fusion), channel_id=1, source_target_pairs={{0,8},{8,16},{16,24},{24,32},{32,40},{40,48},{48,56},{56,64},{64,7... | collective-permute-start | bytes 3080 | tf_op jit(solution)/shard_map/ppermute | solution.py:21
  6.6 5.5 %collective-permute-start.2 = (s32[256]{0:T(256)S(1)}, s32[256]{0:T(256)S(1)}, u32[]{:S(2)}, u32[]{:S(2)}) collective-permute-start(s32[256]{0:T(256)S(1)} %collective-permute-done), channel_id=1, source_target_pairs={{0,8},{8,16},{16,24},{24,32},{32,40},{40,48},{48,56},{56,64},{64,7... | collective-permute-start | bytes 3080 | tf_op jit(solution)/shard_map/ppermute | solution.py:21
  12.0 5.5 %collective-permute-start.4 = (s32[256]{0:T(256)S(1)}, s32[256]{0:T(256)S(1)}, u32[]{:S(2)}, u32[]{:S(2)}) collective-permute-start(s32[256]{0:T(256)S(1)} %collective-permute-done.2), channel_id=1, source_target_pairs={{0,8},{8,16},{16,24},{24,32},{32,40},{40,48},{48,56},{56,64},{64,7... | collective-permute-start | bytes 3080 | tf_op jit(solution)/shard_map/ppermute | solution.py:21
  17.3 10.6 %copy-start.4 = (bf16[256,384]{0,1:T(8,128)(2,1)}, bf16[256,384]{0,1:T(8,128)(2,1)S(1)}, u32[]{:S(2)}) copy-start(bf16[256,384]{0,1:T(8,128)(2,1)S(1)} %copy.85) | copy-start | bytes 589828
  17.5 52.0 %copy-start.6 = (bf16[256,384]{0,1:T(8,128)(2,1)}, bf16[256,384]{0,1:T(8,128)(2,1)S(1)}, u32[]{:S(2)}) copy-start(bf16[256,384]{0,1:T(8,128)(2,1)S(1)} %copy.90) | copy-start | bytes 589828
  17.5 10.1 %collective-permute-start.6 = (s32[256]{0:T(256)S(1)}, s32[256]{0:T(256)S(1)}, u32[]{:S(2)}, u32[]{:S(2)}) collective-permute-start(s32[256]{0:T(256)S(1)} %collective-permute-done.4), channel_id=1, source_target_pairs={{0,8},{8,16},{16,24},{24,32},{32,40},{40,48},{48,56},{56,64},{64,7... | collective-permute-start | bytes 3080 | tf_op jit(solution)/shard_map/ppermute | solution.py:21
  21.8 5.6 %copy-start.38 = (bf16[256,384]{1,0:T(8,128)(2,1)S(1)}, bf16[256,384]{1,0:T(8,128)(2,1)}, u32[]{:S(2)}) copy-start(bf16[256,384]{1,0:T(8,128)(2,1)} %param.6) | copy-start | bytes 589828
  21.9 11.3 %collective-permute-start.1 = (bf16[2,256,384]{1,2,0:T(8,128)(2,1)S(1)}, bf16[2,256,384]{1,2,0:T(8,128)(2,1)S(1)}, u32[]{:S(2)}, u32[]{:S(2)}) collective-permute-start(bf16[2,256,384]{1,2,0:T(8,128)(2,1)S(1)} %pad_maximum_fusion), channel_id=1, source_target_pairs={{0,8},{8,16},{16,24},{24,32},{32,40},{40,48},{48,56},{56,64},{64,7... | collective-permute-start | bytes 1179656 | tf_op jit(solution)/shard_map/ppermute | solution.py:21
  27.9 41.9 %copy-start.14 = (pred[256,256]{0,1:T(8,128)(4,1)}, pred[256,256]{0,1:T(8,128)(4,1)S(1)}, u32[]{:S(2)}) copy-start(pred[256,256]{0,1:T(8,128)(4,1)S(1)} %get-tuple-element.33) | copy-start | bytes 196612
  27.9 42.2 %copy-start.12 = (pred[256,256]{0,1:T(8,128)(4,1)}, pred[256,256]{0,1:T(8,128)(4,1)S(1)}, u32[]{:S(2)}) copy-start(pred[256,256]{0,1:T(8,128)(4,1)S(1)} %get-tuple-element.34) | copy-start | bytes 196612
  27.9 42.5 %copy-start.10 = (pred[256,256]{0,1:T(8,128)(4,1)}, pred[256,256]{0,1:T(8,128)(4,1)S(1)}, u32[]{:S(2)}) copy-start(pred[256,256]{0,1:T(8,128)(4,1)S(1)} %get-tuple-element.35) | copy-start | bytes 196612
  27.9 42.9 %copy-start.8 = (pred[256,256]{0,1:T(8,128)(4,1)}, pred[256,256]{0,1:T(8,128)(4,1)S(1)}, u32[]{:S(2)}) copy-start(pred[256,256]{0,1:T(8,128)(4,1)S(1)} %get-tuple-element.36) | copy-start | bytes 196612
  33.2 10.6 %collective-permute-start.3 = (bf16[2,256,384]{1,2,0:T(8,128)(2,1)S(1)}, bf16[2,256,384]{1,2,0:T(8,128)(2,1)S(1)}, u32[]{:S(2)}, u32[]{:S(2)}) collective-permute-start(bf16[2,256,384]{1,2,0:T(8,128)(2,1)S(1)} %collective-permute-done.1), channel_id=1, source_target_pairs={{0,8},{8,16},{16,24},{24,32},{32,40},{40,48},{48,56},{56,64},{64,7... | collective-permute-start | bytes 1179656 | tf_op jit(solution)/shard_map/ppermute | solution.py:21
  38.4 31.4 %copy-start.18 = (bf16[1,256,384]{1,2,0:T(8,128)(2,1)}, bf16[1,256,384]{1,2,0:T(8,128)(2,1)S(1)}, u32[]{:S(2)}) copy-start(bf16[1,256,384]{1,2,0:T(8,128)(2,1)S(1)} %get-tuple-element.31) | copy-start | bytes 589828
  43.8 14.0 %collective-permute-start.5 = (bf16[2,256,384]{1,2,0:T(8,128)(2,1)S(1)}, bf16[2,256,384]{1,2,0:T(8,128)(2,1)S(1)}, u32[]{:S(2)}, u32[]{:S(2)}) collective-permute-start(bf16[2,256,384]{1,2,0:T(8,128)(2,1)S(1)} %collective-permute-done.3), channel_id=1, source_target_pairs={{0,8},{8,16},{16,24},{24,32},{32,40},{40,48},{48,56},{56,64},{64,7... | collective-permute-start | bytes 1179656 | tf_op jit(solution)/shard_map/ppermute | solution.py:21
  50.6 19.5 %copy-start.20 = (bf16[1,256,384]{1,2,0:T(8,128)(2,1)}, bf16[1,256,384]{1,2,0:T(8,128)(2,1)S(1)}, u32[]{:S(2)}) copy-start(bf16[1,256,384]{1,2,0:T(8,128)(2,1)S(1)} %get-tuple-element.29) | copy-start | bytes 589828
  57.9 10.3 %collective-permute-start.7 = (bf16[2,256,384]{1,2,0:T(8,128)(2,1)S(1)}, bf16[2,256,384]{1,2,0:T(8,128)(2,1)S(1)}, u32[]{:S(2)}, u32[]{:S(2)}) collective-permute-start(bf16[2,256,384]{1,2,0:T(8,128)(2,1)S(1)} %collective-permute-done.5), channel_id=1, source_target_pairs={{0,8},{8,16},{16,24},{24,32},{32,40},{40,48},{48,56},{56,64},{64,7... | collective-permute-start | bytes 1179656 | tf_op jit(solution)/shard_map/ppermute | solution.py:21
  62.9 7.5 %copy-start.22 = (bf16[1,256,384]{1,2,0:T(8,128)(2,1)}, bf16[1,256,384]{1,2,0:T(8,128)(2,1)S(1)}, u32[]{:S(2)}) copy-start(bf16[1,256,384]{1,2,0:T(8,128)(2,1)S(1)} %get-tuple-element.27) | copy-start | bytes 589828
  68.1 2.6 copy-start.24
  68.8 2.0 copy-start
  81.8 2.0 copy-start.36
  81.8 2.0 copy-start.39
  103.4 1.1 copy-start.21
  107.0 1.1 copy-start.1
  107.0 1.1 copy-start.9
  107.0 1.2 copy-start.25
  121.3 227.5 %collective-permute-start.8 = (bf16[2,256,384]{2,1,0:T(8,128)(2,1)}, bf16[2,256,384]{2,1,0:T(8,128)(2,1)S(1)}, u32[]{:S(2)}, u32[]{:S(2)}) collective-permute-start(bf16[2,256,384]{2,1,0:T(8,128)(2,1)} %pad_maximum_fusion.2), channel_id=1, source_target_pairs={{8,0},{16,8},{24,16},{32,24},{40,32},{48,40},{56,48},{64,56},{72,6... | collective-permute-start | bytes 1179656 | tf_op jit(solution)/shard_map/ppermute | solution.py:21
  123.4 225.4 %collective-permute-start.9 = (bf16[2,256,384]{2,1,0:T(8,128)(2,1)}, bf16[2,256,384]{2,1,0:T(8,128)(2,1)S(1)}, u32[]{:S(2)}, u32[]{:S(2)}) collective-permute-start(bf16[2,256,384]{2,1,0:T(8,128)(2,1)} %pad_maximum_fusion.3), channel_id=1, source_target_pairs={{16,0},{24,8},{32,16},{40,24},{48,32},{56,40},{64,48},{72,56},{80,... | collective-permute-start | bytes 1179656 | tf_op jit(solution)/shard_map/ppermute | solution.py:21
  125.5 3.5 %copy-start.17 = (bf16[1,256,384]{1,2,0:T(8,128)(2,1)S(1)}, bf16[1,256,384]{1,2,0:T(8,128)(2,1)}, u32[]{:S(2)}) copy-start(bf16[1,256,384]{1,2,0:T(8,128)(2,1)} %copy-done.16) | copy-start | bytes 589828
  125.5 223.3 %collective-permute-start.11 = (bf16[2,256,384]{2,1,0:T(8,128)(2,1)}, bf16[2,256,384]{2,1,0:T(8,128)(2,1)S(1)}, u32[]{:S(2)}, u32[]{:S(2)}) collective-permute-start(bf16[2,256,384]{2,1,0:T(8,128)(2,1)} %pad_maximum_fusion.5), channel_id=1, source_target_pairs={{32,0},{40,8},{48,16},{56,24},{64,32},{72,40},{80,48},{88,56},{96,... | collective-permute-start | bytes 1179656 | tf_op jit(solution)/shard_map/ppermute | solution.py:21
  127.7 221.1 %collective-permute-start.10 = (bf16[2,256,384]{2,1,0:T(8,128)(2,1)}, bf16[2,256,384]{2,1,0:T(8,128)(2,1)}, u32[]{:S(2)}, u32[]{:S(2)}) collective-permute-start(bf16[2,256,384]{2,1,0:T(8,128)(2,1)} %pad_maximum_fusion.4), channel_id=1, source_target_pairs={{24,0},{32,8},{40,16},{48,24},{56,32},{64,40},{72,48},{80,56},{88,... | collective-permute-start | bytes 1179656 | tf_op jit(solution)/shard_map/ppermute | solution.py:21
  (21 other events, 19.1 us)
where the time goes:
time: 352 us; the launch traced here: 351 us
  blocking collectives  239 us (68%)
  starting transfers between devices  44.2 us (13%)
  waiting for transfers between devices  23.4 us (7%)
  local copies, waits for them, and re-layouts  16.8 us (5%)
  matrix products  14 us (4%)
  other arithmetic  11.7 us (3%)
    psum x1, blocking collectives, body(): lax.psum(jnp.sum(grad_rows * flat_att * rms_inv[:, None], axis=0), 'tm')  217 us
    ppermute x12, starting transfers between devices, passed_along(): return lax.ppermute(x, axis, pairs)  44.2 us
    ppermute x12, waiting for transfers between devices, passed_along(): return lax.ppermute(x, axis, pairs)  23.4 us
    psum x2, blocking collectives, body(): lax.psum((jnp.sum(flat_att * flat_att, axis=1), jnp.sum(scaled * flat_att...  22 us
    unnamed x86, local copies, waits for them, and re-layouts  11.2 us
  transfers between devices with their start and end apart: 12, of which 6 were waited for; matrix products, arithmetic and copies ran while one was open for 2% of the time, Pallas kernels for 0%

commit v1 on v0

--- a/solution.py
+++ b/solution.py
@@ -173,7 +173,9 @@
     grad_att = (
         rms_inv[:, None] * (scaled - flat_att * (rms_inv * rms_inv * cross_sum / features)[:, None])
     ).astype(jnp.bfloat16)
-    grad_gain = lax.psum(jnp.sum(grad_rows * flat_att * rms_inv[:, None], axis=0), "tm")
+    grad_gain = jnp.sum(
+        lax.all_gather(jnp.sum(grad_rows * flat_att * rms_inv[:, None], axis=0), "tm"), axis=0
+    )
     grad_heads = grad_att.reshape(layout)
     row_delta = jnp.sum(attended.astype(jnp.float32) * grad_heads.astype(jnp.float32), axis=2).T
     zero_heads = jnp.zeros(layout, jnp.float32)

time: 352 us -> 313 us (0.89)
  blocking collectives: 239 us -> 197 us
    psum x1 -> x0, blocking collectives: 217 us -> none  [body(): lax.psum(jnp.sum(grad_rows * flat_att * rms_inv[:, None], axis=0), 'tm')]
    all_gather x0 -> x1, blocking collectives: none -> 175 us  [body(): lax.all_gather(jnp.sum(grad_rows * flat_att * rms_inv[:, None], axis=0),...]
    unnamed x86 -> x95, local copies, waits for them, and re-layouts: 11.2 us -> 9.38 us
  transfers between devices with their start and end apart: 12 -> 12, of which waited for: 6 -> 6; matrix products, arithmetic and copies ran while one was open for 2% -> 3% of each run, Pallas kernels for 0% -> 0%
where the time goes in v1:
time: 313 us; the launch traced here: 310 us
  blocking collectives  197 us (63%)
  starting transfers between devices  44.4 us (14%)
  waiting for transfers between devices  23.4 us (7%)
  local copies, waits for them, and re-layouts  16.9 us (5%)
  matrix products  14.7 us (5%)
  other arithmetic  12.3 us (4%)
    all_gather x1, blocking collectives, body(): lax.all_gather(jnp.sum(grad_rows * flat_att * rms_inv[:, None], axis=0),...  175 us
    ppermute x12, starting transfers between devices, passed_along(): return lax.ppermute(x, axis, pairs)  44.4 us
    ppermute x12, waiting for transfers between devices, passed_along(): return lax.ppermute(x, axis, pairs)  23.4 us
    psum x2, blocking collectives, body(): lax.psum((jnp.sum(flat_att * flat_att, axis=1), jnp.sum(scaled * flat_att...  22 us
    unnamed x95, local copies, waits for them, and re-layouts  9.38 us
  transfers between devices with their start and end apart: 12, of which 6 were waited for; matrix products, arithmetic and copies ran while one was open for 3% of the time, Pallas kernels for 0%

profile of v1, /device:TPU:6, one launch (start us, length us, event | category | flops | bytes accessed | tf_op | source)
XLA Modules:
  0.0 310.1 jit_solution(3753476366251063156)
XLA Ops:
  1.4 3.9 %collective-permute-start = (s32[256]{0:T(256)S(1)}, s32[256]{0:T(256)S(1)}, u32[]{:S(2)}, u32[]{:S(2)}) collective-permute-start(s32[256]{0:T(256)S(1)} %broadcast_bitcast_fusion), channel_id=1, source_target_pairs={{0,8},{8,16},{16,24},{24,32},{32,40},{40,48},{48,56},{56,64},{64,7... | collective-permute-start | bytes 3080 | tf_op jit(solution)/shard_map/ppermute | solution.py:21
  5.3 1.3 collective-permute-done
  6.6 4.2 %collective-permute-start.2 = (s32[256]{0:T(256)S(1)}, s32[256]{0:T(256)S(1)}, u32[]{:S(2)}, u32[]{:S(2)}) collective-permute-start(s32[256]{0:T(256)S(1)} %collective-permute-done), channel_id=1, source_target_pairs={{0,8},{8,16},{16,24},{24,32},{32,40},{40,48},{48,56},{56,64},{64,7... | collective-permute-start | bytes 3080 | tf_op jit(solution)/shard_map/ppermute | solution.py:21
  10.8 1.3 collective-permute-done.2
  12.0 4.2 %collective-permute-start.4 = (s32[256]{0:T(256)S(1)}, s32[256]{0:T(256)S(1)}, u32[]{:S(2)}, u32[]{:S(2)}) collective-permute-start(s32[256]{0:T(256)S(1)} %collective-permute-done.2), channel_id=1, source_target_pairs={{0,8},{8,16},{16,24},{24,32},{32,40},{40,48},{48,56},{56,64},{64,7... | collective-permute-start | bytes 3080 | tf_op jit(solution)/shard_map/ppermute | solution.py:21
  16.2 1.1 copy.152
  17.5 4.3 %collective-permute-start.6 = (s32[256]{0:T(256)S(1)}, s32[256]{0:T(256)S(1)}, u32[]{:S(2)}, u32[]{:S(2)}) collective-permute-start(s32[256]{0:T(256)S(1)} %collective-permute-done.4), channel_id=1, source_target_pairs={{0,8},{8,16},{16,24},{24,32},{32,40},{40,48},{48,56},{56,64},{64,7... | collective-permute-start | bytes 3080 | tf_op jit(solution)/shard_map/ppermute | solution.py:21
  21.9 5.5 %collective-permute-start.1 = (bf16[2,256,384]{1,2,0:T(8,128)(2,1)S(1)}, bf16[2,256,384]{1,2,0:T(8,128)(2,1)S(1)}, u32[]{:S(2)}, u32[]{:S(2)}) collective-permute-start(bf16[2,256,384]{1,2,0:T(8,128)(2,1)S(1)} %pad_maximum_fusion), channel_id=1, source_target_pairs={{0,8},{8,16},{16,24},{24,32},{32,40},{40,48},{48,56},{56,64},{64,7... | collective-permute-start | bytes 1179656 | tf_op jit(solution)/shard_map/ppermute | solution.py:21
  28.4 4.8 %collective-permute-done.1 = bf16[2,256,384]{1,2,0:T(8,128)(2,1)S(1)} collective-permute-done((bf16[2,256,384]{1,2,0:T(8,128)(2,1)S(1)}, bf16[2,256,384]{1,2,0:T(8,128)(2,1)S(1)}, u32[]{:S(2)}, u32[]{:S(2)}) %collective-permute-start.1) | collective-permute-done | bytes 393248 | tf_op jit(solution)/shard_map/ppermute | solution.py:21
  33.2 5.1 %collective-permute-start.3 = (bf16[2,256,384]{1,2,0:T(8,128)(2,1)S(1)}, bf16[2,256,384]{1,2,0:T(8,128)(2,1)S(1)}, u32[]{:S(2)}, u32[]{:S(2)}) collective-permute-start(bf16[2,256,384]{1,2,0:T(8,128)(2,1)S(1)} %collective-permute-done.1), channel_id=1, source_target_pairs={{0,8},{8,16},{16,24},{24,32},{32,40},{40,48},{48,56},{56,64},{64,7... | collective-permute-start | bytes 1179656 | tf_op jit(solution)/shard_map/ppermute | solution.py:21
  39.0 4.8 %collective-permute-done.3 = bf16[2,256,384]{1,2,0:T(8,128)(2,1)S(1)} collective-permute-done((bf16[2,256,384]{1,2,0:T(8,128)(2,1)S(1)}, bf16[2,256,384]{1,2,0:T(8,128)(2,1)S(1)}, u32[]{:S(2)}, u32[]{:S(2)}) %collective-permute-start.3) | collective-permute-done | bytes 393248 | tf_op jit(solution)/shard_map/ppermute | solution.py:21
  43.8 6.7 %collective-permute-start.5 = (bf16[2,256,384]{1,2,0:T(8,128)(2,1)S(1)}, bf16[2,256,384]{1,2,0:T(8,128)(2,1)S(1)}, u32[]{:S(2)}, u32[]{:S(2)}) collective-permute-start(bf16[2,256,384]{1,2,0:T(8,128)(2,1)S(1)} %collective-permute-done.3), channel_id=1, source_target_pairs={{0,8},{8,16},{16,24},{24,32},{32,40},{40,48},{48,56},{56,64},{64,7... | collective-permute-start | bytes 1179656 | tf_op jit(solution)/shard_map/ppermute | solution.py:21
  51.2 6.6 %collective-permute-done.5 = bf16[2,256,384]{1,2,0:T(8,128)(2,1)S(1)} collective-permute-done((bf16[2,256,384]{1,2,0:T(8,128)(2,1)S(1)}, bf16[2,256,384]{1,2,0:T(8,128)(2,1)S(1)}, u32[]{:S(2)}, u32[]{:S(2)}) %collective-permute-start.5) | collective-permute-done | bytes 393248 | tf_op jit(solution)/shard_map/ppermute | solution.py:21
  57.9 5.0 %collective-permute-start.7 = (bf16[2,256,384]{1,2,0:T(8,128)(2,1)S(1)}, bf16[2,256,384]{1,2,0:T(8,128)(2,1)S(1)}, u32[]{:S(2)}, u32[]{:S(2)}) collective-permute-start(bf16[2,256,384]{1,2,0:T(8,128)(2,1)S(1)} %collective-permute-done.5), channel_id=1, source_target_pairs={{0,8},{8,16},{16,24},{24,32},{32,40},{40,48},{48,56},{56,64},{64,7... | collective-permute-start | bytes 1179656 | tf_op jit(solution)/shard_map/ppermute | solution.py:21
  63.6 4.5 %collective-permute-done.7 = bf16[2,256,384]{1,2,0:T(8,128)(2,1)S(1)} collective-permute-done((bf16[2,256,384]{1,2,0:T(8,128)(2,1)S(1)}, bf16[2,256,384]{1,2,0:T(8,128)(2,1)S(1)}, u32[]{:S(2)}, u32[]{:S(2)}) %collective-permute-start.7) | collective-permute-done | bytes 393248 | tf_op jit(solution)/shard_map/ppermute | solution.py:21
  70.8 1.1 multiply_reduce_fusion.1
  71.8 10.0 %psum.14 = f32[256]{0:T(256)S(1)} all-reduce(f32[256]{0:T(256)S(1)} %get-tuple-element.53), channel_id=1, replica_groups=mesh['tm'=64,'head'=8] {'head'}, use_global_device_ids=true, to_apply=%region_11.12 | all-reduce | flops 256 | bytes 2048 | tf_op jit(solution)/shard_map/psum | solution.py:168
  81.8 2.0 copy.172
  83.8 1.7 fusion.47
  85.5 12.0 %psum.15 = f32[256]{0:T(256)} all-reduce(f32[256]{0:T(256)} %get-tuple-element.21), channel_id=1, replica_groups=mesh['tm'=64,'head'=8] {'head'}, use_global_device_ids=true, to_apply=%region_13.14 | all-reduce | flops 256 | bytes 2048 | tf_op jit(solution)/shard_map/psum | solution.py:168
  98.3 1.9 fusion.45
  100.2 1.1 copy.175
  101.2 1.1 multiply_reduce_fusion
  103.4 1.1 fusion.11
  104.5 1.1 fusion.12
  107.0 1.0 convolution_convert_fusion.1
  122.2 1.4 collective-permute-start.8
  124.5 1.3 collective-permute-start.9
  126.6 1.4 collective-permute-start.11
  128.8 1.4 collective-permute-start.10
  132.4 174.9 %all-gather.1 = f32[64,1,384]{2,1,0:T(1,128)S(1)} all-gather(f32[1,1,384]{2,1,0:T(1,128)S(1)} %reshape.258), channel_id=2, replica_groups=mesh['tm'=64,'head'=8] {'tm'}, dimensions={0}, use_global_device_ids=true | all-gather | bytes 99840 | tf_op jit(solution)/shard_map/all_gather | solution.py:177
  308.1 1.2 add_convert_fusion
  (158 shorter events, 29.6 us)
Async XLA Ops:
  1.4 15.9 %copy-start.41 = (bf16[256,384]{1,0:T(8,128)(2,1)S(1)}, bf16[256,384]{1,0:T(8,128)(2,1)}, u32[]{:S(2)}) copy-start(bf16[256,384]{1,0:T(8,128)(2,1)} %param.8) | copy-start | bytes 589828
  1.4 5.2 %collective-permute-start = (s32[256]{0:T(256)S(1)}, s32[256]{0:T(256)S(1)}, u32[]{:S(2)}, u32[]{:S(2)}) collective-permute-start(s32[256]{0:T(256)S(1)} %broadcast_bitcast_fusion), channel_id=1, source_target_pairs={{0,8},{8,16},{16,24},{24,32},{32,40},{40,48},{48,56},{56,64},{64,7... | collective-permute-start | bytes 3080 | tf_op jit(solution)/shard_map/ppermute | solution.py:21
  6.6 5.5 %collective-permute-start.2 = (s32[256]{0:T(256)S(1)}, s32[256]{0:T(256)S(1)}, u32[]{:S(2)}, u32[]{:S(2)}) collective-permute-start(s32[256]{0:T(256)S(1)} %collective-permute-done), channel_id=1, source_target_pairs={{0,8},{8,16},{16,24},{24,32},{32,40},{40,48},{48,56},{56,64},{64,7... | collective-permute-start | bytes 3080 | tf_op jit(solution)/shard_map/ppermute | solution.py:21
  12.0 5.5 %collective-permute-start.4 = (s32[256]{0:T(256)S(1)}, s32[256]{0:T(256)S(1)}, u32[]{:S(2)}, u32[]{:S(2)}) collective-permute-start(s32[256]{0:T(256)S(1)} %collective-permute-done.2), channel_id=1, source_target_pairs={{0,8},{8,16},{16,24},{24,32},{32,40},{40,48},{48,56},{56,64},{64,7... | collective-permute-start | bytes 3080 | tf_op jit(solution)/shard_map/ppermute | solution.py:21
  17.3 10.6 %copy-start.4 = (bf16[256,384]{0,1:T(8,128)(2,1)}, bf16[256,384]{0,1:T(8,128)(2,1)S(1)}, u32[]{:S(2)}) copy-start(bf16[256,384]{0,1:T(8,128)(2,1)S(1)} %copy.152) | copy-start | bytes 589828
  17.5 52.0 %copy-start.6 = (bf16[256,384]{0,1:T(8,128)(2,1)}, bf16[256,384]{0,1:T(8,128)(2,1)S(1)}, u32[]{:S(2)}) copy-start(bf16[256,384]{0,1:T(8,128)(2,1)S(1)} %copy.157) | copy-start | bytes 589828
  17.5 10.1 %collective-permute-start.6 = (s32[256]{0:T(256)S(1)}, s32[256]{0:T(256)S(1)}, u32[]{:S(2)}, u32[]{:S(2)}) collective-permute-start(s32[256]{0:T(256)S(1)} %collective-permute-done.4), channel_id=1, source_target_pairs={{0,8},{8,16},{16,24},{24,32},{32,40},{40,48},{48,56},{56,64},{64,7... | collective-permute-start | bytes 3080 | tf_op jit(solution)/shard_map/ppermute | solution.py:21
  21.8 5.6 %copy-start.42 = (bf16[256,384]{1,0:T(8,128)(2,1)S(1)}, bf16[256,384]{1,0:T(8,128)(2,1)}, u32[]{:S(2)}) copy-start(bf16[256,384]{1,0:T(8,128)(2,1)} %param.6) | copy-start | bytes 589828
  21.9 11.3 %collective-permute-start.1 = (bf16[2,256,384]{1,2,0:T(8,128)(2,1)S(1)}, bf16[2,256,384]{1,2,0:T(8,128)(2,1)S(1)}, u32[]{:S(2)}, u32[]{:S(2)}) collective-permute-start(bf16[2,256,384]{1,2,0:T(8,128)(2,1)S(1)} %pad_maximum_fusion), channel_id=1, source_target_pairs={{0,8},{8,16},{16,24},{24,32},{32,40},{40,48},{48,56},{56,64},{64,7... | collective-permute-start | bytes 1179656 | tf_op jit(solution)/shard_map/ppermute | solution.py:21
  27.9 41.9 %copy-start.14 = (pred[256,256]{0,1:T(8,128)(4,1)}, pred[256,256]{0,1:T(8,128)(4,1)S(1)}, u32[]{:S(2)}) copy-start(pred[256,256]{0,1:T(8,128)(4,1)S(1)} %get-tuple-element.38) | copy-start | bytes 196612
  27.9 42.2 %copy-start.12 = (pred[256,256]{0,1:T(8,128)(4,1)}, pred[256,256]{0,1:T(8,128)(4,1)S(1)}, u32[]{:S(2)}) copy-start(pred[256,256]{0,1:T(8,128)(4,1)S(1)} %get-tuple-element.39) | copy-start | bytes 196612
  27.9 42.5 %copy-start.10 = (pred[256,256]{0,1:T(8,128)(4,1)}, pred[256,256]{0,1:T(8,128)(4,1)S(1)}, u32[]{:S(2)}) copy-start(pred[256,256]{0,1:T(8,128)(4,1)S(1)} %get-tuple-element.40) | copy-start | bytes 196612
  27.9 42.8 %copy-start.8 = (pred[256,256]{0,1:T(8,128)(4,1)}, pred[256,256]{0,1:T(8,128)(4,1)S(1)}, u32[]{:S(2)}) copy-start(pred[256,256]{0,1:T(8,128)(4,1)S(1)} %get-tuple-element.41) | copy-start | bytes 196612
  33.2 10.6 %collective-permute-start.3 = (bf16[2,256,384]{1,2,0:T(8,128)(2,1)S(1)}, bf16[2,256,384]{1,2,0:T(8,128)(2,1)S(1)}, u32[]{:S(2)}, u32[]{:S(2)}) collective-permute-start(bf16[2,256,384]{1,2,0:T(8,128)(2,1)S(1)} %collective-permute-done.1), channel_id=1, source_target_pairs={{0,8},{8,16},{16,24},{24,32},{32,40},{40,48},{48,56},{56,64},{64,7... | collective-permute-start | bytes 1179656 | tf_op jit(solution)/shard_map/ppermute | solution.py:21
  38.4 31.4 %copy-start.18 = (bf16[1,256,384]{1,2,0:T(8,128)(2,1)}, bf16[1,256,384]{1,2,0:T(8,128)(2,1)S(1)}, u32[]{:S(2)}) copy-start(bf16[1,256,384]{1,2,0:T(8,128)(2,1)S(1)} %get-tuple-element.36) | copy-start | bytes 589828
  43.8 14.0 %collective-permute-start.5 = (bf16[2,256,384]{1,2,0:T(8,128)(2,1)S(1)}, bf16[2,256,384]{1,2,0:T(8,128)(2,1)S(1)}, u32[]{:S(2)}, u32[]{:S(2)}) collective-permute-start(bf16[2,256,384]{1,2,0:T(8,128)(2,1)S(1)} %collective-permute-done.3), channel_id=1, source_target_pairs={{0,8},{8,16},{16,24},{24,32},{32,40},{40,48},{48,56},{56,64},{64,7... | collective-permute-start | bytes 1179656 | tf_op jit(solution)/shard_map/ppermute | solution.py:21
  50.6 19.5 %copy-start.20 = (bf16[1,256,384]{1,2,0:T(8,128)(2,1)}, bf16[1,256,384]{1,2,0:T(8,128)(2,1)S(1)}, u32[]{:S(2)}) copy-start(bf16[1,256,384]{1,2,0:T(8,128)(2,1)S(1)} %get-tuple-element.34) | copy-start | bytes 589828
  57.9 10.3 %collective-permute-start.7 = (bf16[2,256,384]{1,2,0:T(8,128)(2,1)S(1)}, bf16[2,256,384]{1,2,0:T(8,128)(2,1)S(1)}, u32[]{:S(2)}, u32[]{:S(2)}) collective-permute-start(bf16[2,256,384]{1,2,0:T(8,128)(2,1)S(1)} %collective-permute-done.5), channel_id=1, source_target_pairs={{0,8},{8,16},{16,24},{24,32},{32,40},{40,48},{48,56},{56,64},{64,7... | collective-permute-start | bytes 1179656 | tf_op jit(solution)/shard_map/ppermute | solution.py:21
  62.9 7.5 %copy-start.22 = (bf16[1,256,384]{1,2,0:T(8,128)(2,1)}, bf16[1,256,384]{1,2,0:T(8,128)(2,1)S(1)}, u32[]{:S(2)}) copy-start(bf16[1,256,384]{1,2,0:T(8,128)(2,1)S(1)} %get-tuple-element.32) | copy-start | bytes 589828
  68.1 2.6 copy-start.24
  68.8 2.0 copy-start
  81.8 2.0 copy-start.40
  81.8 2.0 copy-start.43
  107.0 1.2 copy-start.25
  121.5 2.2 copy-start.37
  122.2 3.5 %copy-start.36 = (bf16[1,256,384]{2,1,0:T(8,128)(2,1)S(1)}, bf16[1,256,384]{2,1,0:T(8,128)(2,1)}, u32[]{:S(2)}) copy-start(bf16[1,256,384]{2,1,0:T(8,128)(2,1)} %copy.215) | copy-start | bytes 589828
  122.2 185.8 %collective-permute-start.8 = (bf16[2,256,384]{2,1,0:T(8,128)(2,1)}, bf16[2,256,384]{2,1,0:T(8,128)(2,1)S(1)}, u32[]{:S(2)}, u32[]{:S(2)}) collective-permute-start(bf16[2,256,384]{2,1,0:T(8,128)(2,1)} %pad_maximum_fusion.2), channel_id=1, source_target_pairs={{8,0},{16,8},{24,16},{32,24},{40,32},{48,40},{56,48},{64,56},{72,6... | collective-permute-start | bytes 1179656 | tf_op jit(solution)/shard_map/ppermute | solution.py:21
  124.5 183.6 %collective-permute-start.9 = (bf16[2,256,384]{2,1,0:T(8,128)(2,1)}, bf16[2,256,384]{2,1,0:T(8,128)(2,1)S(1)}, u32[]{:S(2)}, u32[]{:S(2)}) collective-permute-start(bf16[2,256,384]{2,1,0:T(8,128)(2,1)} %pad_maximum_fusion.3), channel_id=1, source_target_pairs={{16,0},{24,8},{32,16},{40,24},{48,32},{56,40},{64,48},{72,56},{80,... | collective-permute-start | bytes 1179656 | tf_op jit(solution)/shard_map/ppermute | solution.py:21
  126.6 3.7 %copy-start.17 = (bf16[1,256,384]{1,2,0:T(8,128)(2,1)S(1)}, bf16[1,256,384]{1,2,0:T(8,128)(2,1)}, u32[]{:S(2)}) copy-start(bf16[1,256,384]{1,2,0:T(8,128)(2,1)} %copy-done.16) | copy-start | bytes 589828
  126.6 181.5 %collective-permute-start.11 = (bf16[2,256,384]{2,1,0:T(8,128)(2,1)}, bf16[2,256,384]{2,1,0:T(8,128)(2,1)S(1)}, u32[]{:S(2)}, u32[]{:S(2)}) collective-permute-start(bf16[2,256,384]{2,1,0:T(8,128)(2,1)} %pad_maximum_fusion.5), channel_id=1, source_target_pairs={{32,0},{40,8},{48,16},{56,24},{64,32},{72,40},{80,48},{88,56},{96,... | collective-permute-start | bytes 1179656 | tf_op jit(solution)/shard_map/ppermute | solution.py:21
  128.8 2.1 copy-start.32
  128.8 179.3 %collective-permute-start.10 = (bf16[2,256,384]{2,1,0:T(8,128)(2,1)}, bf16[2,256,384]{2,1,0:T(8,128)(2,1)}, u32[]{:S(2)}, u32[]{:S(2)}) collective-permute-start(bf16[2,256,384]{2,1,0:T(8,128)(2,1)} %pad_maximum_fusion.4), channel_id=1, source_target_pairs={{24,0},{32,8},{40,16},{48,24},{56,32},{64,40},{72,48},{80,56},{88,... | collective-permute-start | bytes 1179656 | tf_op jit(solution)/shard_map/ppermute | solution.py:21
  (25 other events, 23.4 us)
